TPU v7x, 32 devices: a whole 2x2x4 slice. The times are simulated.
32 devices in a mesh: grp: 4 (over z), mem: 8 (over y, x, core).
Axes of the slice: x: 2, y: 2, z: 4, core: 2. Of those that a mesh axis runs over, the one named last changes fastest.
Arguments:
- volume: float32 [4, 8, 8, 512, 1024], P('grp', 'mem'), may hold values from -1 to 1
- transfer_coef: float32 [4, 4], replicated, may hold values from -3 to 3
- group_order: int32 [4], replicated, may hold values from 0 to 3, each once
- member_order: int32 [4, 8], replicated, may hold values from 0 to 7, each once within a row
- active_mask: int32 [4, 8], P('grp', 'mem'), may hold values 0 or 1
Outputs:
- picture: float32 [4, 512, 1024], P(None, 'mem', 'grp')
All inputs are finite; a program needn't handle non-finite values. No bound on the sum of `active_mask` on one device may be relied on, other than what follows from the above.
Results may differ from a plain program's by a relative error of at most 0.0003.
Values sent between devices are 32-bit elements; how exact they have to be, the bound alone decides.
A program may use at most 192 MiB of HBM per device.

v0:
```python
import jax
import jax.numpy as jnp
from jax import lax
from jax.sharding import PartitionSpec as P


def polynomial(coef_row, values):
    return coef_row[0] + values * (coef_row[1] + values * (coef_row[2] + values * coef_row[3]))


def march_brick(samples, transfer_coef, active_flag, density_scale):
    optical_depth = jnp.zeros(samples.shape[1:], jnp.float32)
    colour = jnp.zeros((3,) + samples.shape[1:], jnp.float32)
    for sample_index in range(samples.shape[0]):
        values = samples[sample_index]
        extinction = polynomial(transfer_coef[3], values) ** 2 * density_scale
        opacity = 1.0 - jnp.exp(-extinction)
        tinted = jax.nn.sigmoid(
            jnp.stack([polynomial(transfer_coef[channel], values) for channel in range(3)])
        )
        colour = colour + (jnp.exp(-optical_depth) * opacity)[None] * tinted
        optical_depth = optical_depth + extinction
    coverage = 1.0 - jnp.exp(-optical_depth)
    return jnp.concatenate([colour, coverage[None]], 0) * active_flag


def reorder(layers, rank_list):
    total = rank_list.shape[0]
    positions = jnp.arange(total, dtype=jnp.int32)
    inverse = jnp.sum(
        positions[:, None] * (rank_list[:, None] == positions[None, :]).astype(jnp.int32), axis=0
    )
    return jnp.take(layers, inverse, axis=0)


def over_tree(layers):
    while layers.shape[0] > 1:
        nearer = layers[0::2]
        farther = layers[1::2]
        layers = nearer + (1.0 - nearer[:, 3:4]) * farther
    return layers[0]


def body(volume, transfer_coef, group_order, member_order, active_mask):
    groups = lax.axis_size("grp")
    members = lax.axis_size("mem")
    density_scale = 3.0 / (volume.shape[2] * groups * members)
    active_flag = active_mask[0, 0].astype(jnp.float32)
    layer = march_brick(volume[0, 0], transfer_coef, active_flag, density_scale)
    slab_ranks = lax.dynamic_slice_in_dim(member_order, lax.axis_index("grp"), 1, 0)[0]
    slab_image = over_tree(
        reorder(
            lax.all_to_all(layer[None], "mem", split_axis=2, concat_axis=0, tiled=True), slab_ranks
        )
    )
    return over_tree(
        reorder(
            lax.all_to_all(slab_image[None], "grp", split_axis=3, concat_axis=0, tiled=True),
            group_order,
        )
    )


def solution(mesh):
    in_specs = (P("grp", "mem", None, None, None), P(), P(), P(), P("grp", "mem"))
    out_specs = P(None, "mem", "grp")
    return jax.shard_map(body, mesh=mesh, in_specs=in_specs, out_specs=out_specs, check_vma=False)
```

profile of v0, /device:TPU:2, one launch (start us, length us, event | category | flops | bytes accessed | tf_op | source)
XLA Modules:
  0.0 448.7 jit_solution(17760567947958751179)
XLA Ops:
  0.0 6.7 %slice_bitcast_fusion = (f32[1,512,1024]{2,1,0:T(8,128)S(1)}, f32[1,1,1,512,1024]{4,3,2,1,0:T(8,128)S(1)}, f32[1,1,1,512,1024]{4,3,2,1,0:T(8,128)S(1)}, f32[1,1,...) fusion(f32[1,1,8,512,1024]{4,3,2,1,0:T(8,128)} %param.5), kind=kLoop, calls=%fused_computation.159 | loop fusion | bytes 33554432 | tf_op jit(solution)/shard_map/squeeze | solution.py:15
  6.7 0.9 fusion.105
  7.6 31.3 %multiply_add_fusion.4 = (f32[1,512,1024]{2,0,1:T(1,128)}, f32[1,512,1024]{2,0,1:T(1,128)}, f32[1,512,1024]{2,0,1:T(1,128)}, f32[1,512,1024]{2,0,1:T(1,128)}, f3...) fusion(f32[]{:T(128)} %bitcast.9, f32[]{:T(128)} %bitcast.8, f32[]{:T(128)} %bitcast.7, f32[]{:T(128)} %bitcast.6, ...), kind=kLoop, calls=%fused_computation.130 | loop fusion | flops 18874368 | bytes 16777264 | tf_op jit(solution)/shard_map/add | solution.py:8
  39.0 30.7 %multiply_add_fusion.10 = (f32[1,512,1024]{2,0,1:T(1,128)}, f32[1,512,1024]{2,0,1:T(1,128)}, f32[1,512,1024]{2,0,1:T(1,128)}, f32[1,512,1024]{2,0,1:T(1,128)}, f...) fusion(f32[1,1,1,512,1024]{4,3,2,1,0:T(8,128)S(1)} %get-tuple-element.16, f32[]{:T(128)} %bitcast.9, f32[]{:T(128)} %bitcast.8, ...), kind=kLoop, calls=%fused_computation.137 | loop fusion | flops 18874368 | bytes 16777264 | tf_op jit(solution)/shard_map/add | solution.py:8
  69.6 30.7 %multiply_add_fusion.16 = (f32[1,512,1024]{2,0,1:T(1,128)}, f32[1,512,1024]{2,0,1:T(1,128)}, f32[1,512,1024]{2,0,1:T(1,128)}, f32[1,512,1024]{2,0,1:T(1,128)}, f...) fusion(f32[1,1,1,512,1024]{4,3,2,1,0:T(8,128)S(1)} %get-tuple-element.18, f32[]{:T(128)} %bitcast.9, f32[]{:T(128)} %bitcast.8, ...), kind=kLoop, calls=%fused_computation.145 | loop fusion | flops 18874368 | bytes 16777264 | tf_op jit(solution)/shard_map/add | solution.py:8
  100.3 32.0 %multiply_add_fusion.22 = (f32[1,512,1024]{2,0,1:T(1,128)}, f32[1,512,1024]{2,0,1:T(1,128)}, f32[1,512,1024]{2,0,1:T(1,128)}, f32[1,512,1024]{2,0,1:T(1,128)}, f...) fusion(f32[1,1,1,512,1024]{4,3,2,1,0:T(8,128)S(1)} %get-tuple-element.20, f32[]{:T(128)} %bitcast.9, f32[]{:T(128)} %bitcast.8, ...), kind=kLoop, calls=%fused_computation.153 | loop fusion | flops 18874368 | bytes 16777264 | tf_op jit(solution)/shard_map/add | solution.py:8
  132.3 41.6 %fusion.86 = f32[1,1,512,1024]{3,1,0,2:T(1,128)} fusion(f32[1,1,1,512,1024]{4,3,2,1,0:T(8,128)S(1)} %get-tuple-element.16, f32[1,1,1,512,1024]{4,3,2,1,0:T(8,128)S(1)} %get-tuple-element.17, f32[1,1,1,512,1024]{4,3,2,1,0:T(8,128)S(1)} %get-tuple-element.18, f32[1,1,1,512,1024]{4,3,2,1,0:T(8,128)S(1)} %get-tuple-element.19, ...), kind=kLoop, calls=%fused_computation.126 | loop fusion | flops 34603008 | bytes 18874384 | tf_op jit(solution)/shard_map/concatenate | solution.py:24
  174.0 6.2 %subtract_multiply_fusion.3 = (f32[512,1024]{1,0:T(8,128)}, f32[512,1024]{1,0:T(8,128)S(1)}) fusion(f32[]{:T(128)} %bitcast.5, f32[]{:T(128)} %bitcast.4, f32[]{:T(128)} %bitcast.3, f32[]{:T(128)} %bitcast.1, f32[1,1,8,512,1024]{4,3,2,1,0:T(8,128)S(1)} %bitcast.282), kind=kLoop, calls=%fused_computation.146 | loop fusion | flops 19922944 | bytes 12582928 | tf_op jit(solution)/shard_map/mul | solution.py:21
  180.2 6.7 %subtract_multiply_fusion.1 = (f32[512,1024]{1,0:T(8,128)}, f32[512,1024]{1,0:T(8,128)S(1)}, f32[512,1024]{1,0:T(8,128)}) fusion(f32[]{:T(128)} %bitcast.5, f32[]{:T(128)} %bitcast.4, f32[]{:T(128)} %bitcast.3, f32[]{:T(128)} %bitcast.1, f32[1,1,8,512,1024]{4,3,2,1,0:T(8,128)S(1)} %bitcast.282, f32[512,1024]{1,0:T(8,128)S(1)} %get-tuple-element.6), kind=kLoop, calls=%fused_computation.138 | loop fusion | flops 17825792 | bytes 14680080 | tf_op jit(solution)/shard_map/mul | solution.py:21
  187.0 11.5 %subtract_multiply_fusion = (f32[512,1024]{1,0:T(8,128)}, f32[512,1024]{1,0:T(8,128)}, f32[512,1024]{1,0:T(8,128)}, f32[512,1024]{1,0:T(8,128)}, f32[512,1024]{1,0:T(8,128)}) fusion(f32[]{:T(128)} %bitcast.5, f32[]{:T(128)} %bitcast.4, f32[]{:T(128)} %bitcast.3, f32[]{:T(128)} %bitcast.1, f32[512,1024]{1,0:T(8,128)S(1)} %get-tuple-element.8, ...), kind=kLoop, calls=%fused_computation.134 | loop fusion | flops 35651584 | bytes 25165840 | tf_op jit(solution)/shard_map/mul | solution.py:21
  199.2 75.1 %fusion.39 = f32[1,3,512,1024]{3,1,0,2:T(4,128)S(1)} fusion(f32[1,512,1024]{2,0,1:T(1,128)S(1)} %copy-done.4, f32[1,512,1024]{2,0,1:T(1,128)S(1)} %copy-done.5, f32[1,512,1024]{2,0,1:T(1,128)S(1)} %copy-done.3, f32[1,512,1024]{2,0,1:T(1,128)S(1)} %copy-done.6, f32[1,512,1024]{2,0,1:T(1,128)S(1)} %copy-done.7, f32[1,512,1024]{2,0,1:T(1,128)S(1)} %copy-done.8, ...), kind=kLoop, calls=%fused_computation.51 | loop fusion | flops 86507520 | bytes 73400320 | tf_op jit(solution)/shard_map/concatenate | solution.py:24
  274.3 7.1 %maximum_multiply_fusion = f32[1,4,512,1024]{3,1,0,2:T(4,128)} fusion(f32[1,1,512,1024]{3,1,0,2:T(1,128)} %fusion.86, f32[1,3,512,1024]{3,1,0,2:T(4,128)S(1)} %fusion.39, f32[]{:T(128)} %bitcast.29), kind=kLoop, calls=%fused_computation.49 | loop fusion | flops 4194304 | bytes 16777220 | tf_op jit(solution)/shard_map/mul | solution.py:24
  281.4 5.1 %all-to-all-start = ((f32[1,4,512,1024]{3,1,0,2:T(4,128)}), f32[1,4,512,1024]{3,1,0,2:T(4,128)}, u32[]{:S(2)}, u32[]{:S(2)}) async-start(f32[1,4,512,1024]{3,1,0,2:T(4,128)} %maximum_multiply_fusion), calls=%async_computation | async-start | bytes 16777216 | tf_op jit(solution)/shard_map/all_to_all | solution.py:53
  286.6 92.2 %all-to-all-done = f32[1,4,512,1024]{3,1,0,2:T(4,128)} async-done(((f32[1,4,512,1024]{3,1,0,2:T(4,128)}), f32[1,4,512,1024]{3,1,0,2:T(4,128)}, u32[]{:S(2)}, u32[]{:S(2)}) %all-to-all-start) | async-done | bytes 8388640 | tf_op jit(solution)/shard_map/all_to_all | solution.py:53
  378.8 11.3 %copy.99 = f32[1,4,8,64,1024]{4,3,1,2,0:T(8,128)} copy(f32[1,4,8,64,1024]{4,1,3,2,0:T(4,128)} %bitcast.30) | data formatting | bytes 16777216 | tf_op jit(solution)/shard_map/all_to_all | solution.py:53
  390.1 7.7 %gather_fusion = f32[8,4,64,1024]{3,2,1,0:T(8,128)} fusion(f32[8,4,64,1024]{3,2,1,0:T(8,128)} %bitcast.283, s32[1024]{0:T(1024)S(1)} %pad_clamp_fusion.1), kind=kCustom, calls=%fused_computation | custom fusion | bytes 16777248 | tf_op jit(solution)/shard_map/jit(_take)/gather | solution.py:33
  397.9 4.4 broadcast_select_fusion
  402.9 1.1 multiply_add_fusion
  405.2 0.9 copy.75
  406.1 2.9 reshape.2041
  409.0 5.4 %all-to-all-start.1 = ((f32[4,1,65536]{2,1,0:T(1,128)}), f32[4,1,65536]{2,1,0:T(1,128)S(1)}, u32[]{:S(2)}, u32[]{:S(2)}) async-start(f32[4,1,65536]{2,1,0:T(1,128)} %reshape.2041), calls=%async_computation.1 | async-start | bytes 2097152 | tf_op jit(solution)/shard_map/all_to_all | solution.py:58
  414.6 25.8 %all-to-all-done.1 = f32[4,1,65536]{2,1,0:T(1,128)S(1)} async-done(((f32[4,1,65536]{2,1,0:T(1,128)}), f32[4,1,65536]{2,1,0:T(1,128)S(1)}, u32[]{:S(2)}, u32[]{:S(2)}) %all-to-all-start.1) | async-done | bytes 1048608 | tf_op jit(solution)/shard_map/all_to_all | solution.py:58
  441.0 3.8 reduce
  444.7 1.4 reshape.2042
  (56 shorter events, 5.0 us)
Async XLA Ops:
  0.0 286.5 %copy-start = (s32[4,8]{1,0:T(4,128)S(1)}, s32[4,8]{1,0:T(4,128)}, u32[]{:S(2)}) copy-start(s32[4,8]{1,0:T(4,128)} %param.8) | copy-start | bytes 388
  0.0 6.7 %copy-start.9 = (f32[4,4]{1,0:T(4,128)S(1)}, f32[4,4]{1,0:T(4,128)}, u32[]{:S(2)}) copy-start(f32[4,4]{1,0:T(4,128)} %param.6) | copy-start | bytes 196
  6.7 32.2 %copy-start.1 = (f32[1,1,1,512,1024]{4,3,2,1,0:T(8,128)}, f32[1,1,1,512,1024]{4,3,2,1,0:T(8,128)S(1)}, u32[]{:S(2)}) copy-start(f32[1,1,1,512,1024]{4,3,2,1,0:T(8,128)S(1)} %get-tuple-element.22) | copy-start | bytes 6291460
  100.3 32.0 %copy-start.2 = (f32[1,1,1,512,1024]{4,3,2,1,0:T(8,128)S(1)}, f32[1,1,1,512,1024]{4,3,2,1,0:T(8,128)}, u32[]{:S(2)}) copy-start(f32[1,1,1,512,1024]{4,3,2,1,0:T(8,128)} %copy-done.1) | copy-start | bytes 6291460
  100.3 73.6 %slice-start = ((s8[16777216]{0:T(1024)(128)(4,1)}), s8[4194304]{0:T(1024)(128)(4,1)S(1)}, s32[]{:S(2)}) async-start(s8[16777216]{0:T(1024)(128)(4,1)} %bitcast.281), calls=%async_computation.2 | async-start | bytes 8388608
  100.3 73.6 %slice-start.1 = ((s8[16777216]{0:T(1024)(128)(4,1)}), s8[4194304]{0:T(1024)(128)(4,1)S(1)}, s32[]{:S(2)}) async-start(s8[16777216]{0:T(1024)(128)(4,1)} %bitcast.281), calls=%async_computation.3 | async-start | bytes 8388608
  132.3 41.6 %slice-start.2 = ((s8[16777216]{0:T(1024)(128)(4,1)}), s8[4194304]{0:T(1024)(128)(4,1)S(1)}, s32[]{:S(2)}) async-start(s8[16777216]{0:T(1024)(128)(4,1)} %bitcast.281), calls=%async_computation.4 | async-start | bytes 8388608
  132.3 41.6 %slice-start.3 = ((s8[16777216]{0:T(1024)(128)(4,1)}), s8[4194304]{0:T(1024)(128)(4,1)S(1)}, s32[]{:S(2)}) async-start(s8[16777216]{0:T(1024)(128)(4,1)} %bitcast.281), calls=%async_computation.5 | async-start | bytes 8388608
  187.0 12.2 %copy-start.3 = (f32[1,512,1024]{2,0,1:T(1,128)S(1)}, f32[1,512,1024]{2,0,1:T(1,128)}, u32[]{:S(2)}) copy-start(f32[1,512,1024]{2,0,1:T(1,128)} %get-tuple-element.44) | copy-start | bytes 6291460
  187.0 12.2 %copy-start.4 = (f32[1,512,1024]{2,0,1:T(1,128)S(1)}, f32[1,512,1024]{2,0,1:T(1,128)}, u32[]{:S(2)}) copy-start(f32[1,512,1024]{2,0,1:T(1,128)} %get-tuple-element.45) | copy-start | bytes 6291460
  187.0 12.2 %copy-start.5 = (f32[1,512,1024]{2,0,1:T(1,128)S(1)}, f32[1,512,1024]{2,0,1:T(1,128)}, u32[]{:S(2)}) copy-start(f32[1,512,1024]{2,0,1:T(1,128)} %get-tuple-element.46) | copy-start | bytes 6291460
  187.0 12.2 %copy-start.6 = (f32[1,512,1024]{2,0,1:T(1,128)S(1)}, f32[1,512,1024]{2,0,1:T(1,128)}, u32[]{:S(2)}) copy-start(f32[1,512,1024]{2,0,1:T(1,128)} %get-tuple-element.63) | copy-start | bytes 6291460
  187.0 12.2 %copy-start.7 = (f32[1,512,1024]{2,0,1:T(1,128)S(1)}, f32[1,512,1024]{2,0,1:T(1,128)}, u32[]{:S(2)}) copy-start(f32[1,512,1024]{2,0,1:T(1,128)} %get-tuple-element.64) | copy-start | bytes 6291460
  187.0 12.2 %copy-start.8 = (f32[1,512,1024]{2,0,1:T(1,128)S(1)}, f32[1,512,1024]{2,0,1:T(1,128)}, u32[]{:S(2)}) copy-start(f32[1,512,1024]{2,0,1:T(1,128)} %get-tuple-element.65) | copy-start | bytes 6291460
  281.4 97.5 %all-to-all-start = ((f32[1,4,512,1024]{3,1,0,2:T(4,128)}), f32[1,4,512,1024]{3,1,0,2:T(4,128)}, u32[]{:S(2)}, u32[]{:S(2)}) async-start(f32[1,4,512,1024]{3,1,0,2:T(4,128)} %maximum_multiply_fusion), calls=%async_computation | async-start | bytes 16777216 | tf_op jit(solution)/shard_map/all_to_all | solution.py:53
  406.1 8.4 %copy-start.10 = (s32[4]{0:T(128)S(1)}, s32[4]{0:T(128)}, u32[]{:S(2)}) copy-start(s32[4]{0:T(128)} %param.7) | copy-start | bytes 52
  409.0 31.4 %all-to-all-start.1 = ((f32[4,1,65536]{2,1,0:T(1,128)}), f32[4,1,65536]{2,1,0:T(1,128)S(1)}, u32[]{:S(2)}, u32[]{:S(2)}) async-start(f32[4,1,65536]{2,1,0:T(1,128)} %reshape.2041), calls=%async_computation.1 | async-start | bytes 2097152 | tf_op jit(solution)/shard_map/all_to_all | solution.py:58
where the time goes:
time: 450 us; the launch traced here: 449 us
  other arithmetic  285 us (63%)
  waiting for transfers between devices  118 us (26%)
  local copies, waits for them, and re-layouts  34.6 us (8%)
  starting transfers between devices  10.6 us (2%)
    add x4, other arithmetic, polynomial(): coef_row[0]  125 us
    concatenate x2, other arithmetic, march_brick(): return jnp.concatenate([colour, coverage[None]], 0) * active_flag  117 us
    all_to_all x1, waiting for transfers between devices, body(): lax.all_to_all(layer[None], 'mem', split_axis=2, concat_axis=0, tiled=True)  92.2 us
    all_to_all x1, waiting for transfers between devices, body(): lax.all_to_all(slab_image[None], 'grp', split_axis=3, concat_axis=0, tile...  25.8 us
    mul x3, other arithmetic, march_brick(): colour = colour + (jnp.exp(-optical_depth) * opacity)[None] * tinted  24.5 us
    all_to_all x1, local copies, waits for them, and re-layouts, body(): lax.all_to_all(layer[None], 'mem', split_axis=2, concat_axis=0, tiled=True)  11.3 us
  transfers between devices with their start and end apart: 2, of which 2 were waited for; matrix products, arithmetic and copies ran while one was open for 0% of the time, Pallas kernels for 0%

commit v1 on v0

--- a/solution.py
+++ b/solution.py
@@ -2,6 +2,22 @@
 import jax.numpy as jnp
 from jax import lax
 from jax.sharding import PartitionSpec as P
+
+
+def exchange_in_pairs(value, axis, split, join):
+    ways, here = (lax.axis_size(axis), lax.axis_index(axis))
+    width = value.shape[split] // ways
+    dims = list(value.shape)
+    dims[split] = width
+    height = dims[join]
+    dims[join] = height * ways
+    full = jnp.zeros(dims, value.dtype)
+    for mask in range(ways):
+        part = lax.dynamic_slice_in_dim(value, (here ^ mask) * width, width, axis=split)
+        if mask:
+            part = lax.ppermute(part, axis, [(d, d ^ mask) for d in range(ways)])
+        full = lax.dynamic_update_slice_in_dim(full, part, (here ^ mask) * height, axis=join)
+    return full
 
 
 def polynomial(coef_row, values):
@@ -48,11 +64,7 @@
     active_flag = active_mask[0, 0].astype(jnp.float32)
     layer = march_brick(volume[0, 0], transfer_coef, active_flag, density_scale)
     slab_ranks = lax.dynamic_slice_in_dim(member_order, lax.axis_index("grp"), 1, 0)[0]
-    slab_image = over_tree(
-        reorder(
-            lax.all_to_all(layer[None], "mem", split_axis=2, concat_axis=0, tiled=True), slab_ranks
-        )
-    )
+    slab_image = over_tree(reorder(exchange_in_pairs(layer[None], "mem", 2, 0), slab_ranks))
     return over_tree(
         reorder(
             lax.all_to_all(slab_image[None], "grp", split_axis=3, concat_axis=0, tiled=True),

time: 450 us -> 281 us (0.62)
  other arithmetic: 285 us -> 126 us
  waiting for transfers between devices: 118 us -> 99 us
  local copies, waits for them, and re-layouts: 34.6 us -> 42.7 us
    concatenate x2 -> x0, other arithmetic: 117 us -> none  [march_brick(): return jnp.concatenate([colour, coverage[None]], 0) * active_flag]
    all_to_all x1 -> x0, waiting for transfers between devices: 92.2 us -> none  [body(): lax.all_to_all(layer[None], 'mem', split_axis=2, concat_axis=0, tiled=True)]
    ppermute x0 -> x7, waiting for transfers between devices: none -> 72.4 us  [exchange_in_pairs(): part = lax.ppermute(part, axis, [(d, d ^ mask) for d in range(ways)])]
    add x4, other arithmetic: 125 us -> 53.3 us  [polynomial(): coef_row[0]]
    add x0 -> x1, other arithmetic: none -> 23.5 us  [march_brick(): colour = colour + (jnp.exp(-optical_depth) * opacity)[None] * tinted]
    dynamic_update_slice x0 -> x8, local copies, waits for them, and re-layouts: none -> 16.2 us  [exchange_in_pairs(): lax.dynamic_update_slice_in_dim(full, part, (here ^ mask) * height, axis=...]
    sub x0 -> x2, other arithmetic: none -> 15.8 us  [the longest x1 8.02 us: march_brick(): opacity = 1.0 - jnp.exp(-extinction)]
    all_to_all x1 -> x0, local copies, waits for them, and re-layouts: 11.3 us -> none  [body(): lax.all_to_all(layer[None], 'mem', split_axis=2, concat_axis=0, tiled=True)]
  transfers between devices with their start and end apart: 2 -> 8, of which waited for: 2 -> 4; matrix products, arithmetic and copies ran while one was open for 0% -> 7% of each run, Pallas kernels for 0% -> 0%
where the time goes in v1:
time: 281 us; the launch traced here: 279 us
  other arithmetic  126 us (45%)
  waiting for transfers between devices  99 us (35%)
  local copies, waits for them, and re-layouts  42.7 us (15%)
  starting transfers between devices  10.2 us (4%)
    ppermute x7, waiting for transfers between devices, exchange_in_pairs(): part = lax.ppermute(part, axis, [(d, d ^ mask) for d in range(ways)])  72.4 us
    add x4, other arithmetic, polynomial(): coef_row[0]  53.3 us
    all_to_all x1, waiting for transfers between devices, body(): lax.all_to_all(slab_image[None], 'grp', split_axis=3, concat_axis=0, tile...  26.7 us
    add x1, other arithmetic, march_brick(): colour = colour + (jnp.exp(-optical_depth) * opacity)[None] * tinted  23.5 us
    mul x2, other arithmetic, march_brick(): colour = colour + (jnp.exp(-optical_depth) * opacity)[None] * tinted  17.1 us
    dynamic_update_slice x8, local copies, waits for them, and re-layouts, exchange_in_pairs(): lax.dynamic_update_slice_in_dim(full, part, (here ^ mask) * height, axis=...  16.2 us
    gather x2, local copies, waits for them, and re-layouts, reorder(): return jnp.take(layers, inverse, axis=0)  8.31 us
    sub x1, other arithmetic, march_brick(): opacity = 1.0 - jnp.exp(-extinction)  8.02 us
  transfers between devices with their start and end apart: 8, of which 4 were waited for; matrix products, arithmetic and copies ran while one was open for 7% of the time, Pallas kernels for 0%

profile of v1, /device:TPU:2, one launch (start us, length us, event | category | flops | bytes accessed | tf_op | source)
XLA Modules:
  0.0 278.7 jit_solution(6859009751352361616)
XLA Ops:
  2.0 16.1 %fusion.41 = (f32[1,512,1024]{2,1,0:T(8,128)S(1)}, f32[1,512,1024]{2,1,0:T(8,128)}, f32[1,512,1024]{2,1,0:T(8,128)}, f32[1,512,1024]{2,1,0:T(8,128)}, f32[1,512,...) fusion(f32[1,1,8,512,1024]{4,3,2,1,0:T(8,128)} %param.5, f32[]{:T(128)} %bitcast.10, f32[]{:T(128)} %bitcast.9, ...), kind=kLoop, calls=%fused_computation.66 | loop fusion | flops 22020096 | bytes 20971568 | tf_op jit(solution)/shard_map/add | solution.py:24
  18.1 13.2 %fusion.44 = (f32[1,512,1024]{2,1,0:T(8,128)}, f32[1,512,1024]{2,1,0:T(8,128)}, f32[1,512,1024]{2,1,0:T(8,128)}, f32[1,512,1024]{2,1,0:T(8,128)}, f32[1,512,1024...) fusion(f32[1,1,8,512,1024]{4,3,2,1,0:T(8,128)S(1)} %copy-done.1, f32[]{:T(128)} %bitcast.14, ...), kind=kLoop, calls=%fused_computation.69 | loop fusion | flops 22020096 | bytes 20971568 | tf_op jit(solution)/shard_map/add | solution.py:24
  31.3 13.2 %fusion.47 = (f32[1,512,1024]{2,1,0:T(8,128)}, f32[1,512,1024]{2,1,0:T(8,128)}, f32[1,512,1024]{2,1,0:T(8,128)}, f32[1,512,1024]{2,1,0:T(8,128)}, f32[1,512,1024...) fusion(f32[1,1,8,512,1024]{4,3,2,1,0:T(8,128)S(1)} %copy-done.1, f32[]{:T(128)} %bitcast.18, ...), kind=kLoop, calls=%fused_computation.72 | loop fusion | flops 22020096 | bytes 20971568 | tf_op jit(solution)/shard_map/add | solution.py:24
  44.5 10.8 %fusion.68 = (f32[1,512,1024]{2,1,0:T(8,128)}, f32[1,512,1024]{2,1,0:T(8,128)}, f32[1,512,1024]{2,1,0:T(8,128)}) fusion(f32[1,1,8,512,1024]{4,3,2,1,0:T(8,128)S(1)} %copy-done.1, f32[]{:T(128)} %bitcast.10, f32[]{:T(128)} %bitcast.9, f32[]{:T(128)} %bitcast.8, f32[]{:T(128)} %bitcast.6, f32[]{:T(128)} %bitcast.18, f32[]{:T(128)} %bitcast.17, f32[]{:T(128)} %bitcast.16, ...), kind=kLoop, calls=%fused_computation.108 | loop fusion | flops 9437184 | bytes 8388656 | tf_op jit(solution)/shard_map/add | solution.py:24
  55.3 8.0 %fusion.198 = (f32[512,1024]{1,0:T(8,128)}, f32[512,1024]{1,0:T(8,128)}, f32[512,1024]{1,0:T(8,128)}, f32[512,1024]{1,0:T(8,128)}, f32[512,1024]{1,0:T(8,128)}) fusion(f32[]{:T(128)} %bitcast.5, f32[]{:T(128)} %bitcast.4, f32[]{:T(128)} %bitcast.3, f32[1,1,8,512,1024]{4,3,2,1,0:T(8,128)S(1)} %copy-done.1, f32[]{:T(128)} %bitcast.1), kind=kLoop, calls=%fused_computation.339 | loop fusion | flops 24641536 | bytes 18874384 | tf_op jit(solution)/shard_map/sub | solution.py:33
  63.3 7.8 %fusion.56 = f32[1,512,1024]{2,1,0:T(8,128)} fusion(f32[1,1,8,512,1024]{4,3,2,1,0:T(8,128)S(1)} %copy-done.1, f32[]{:T(128)} %bitcast.5, f32[]{:T(128)} %bitcast.4, f32[]{:T(128)} %bitcast.3, f32[]{:T(128)} %bitcast.1), kind=kLoop, calls=%fused_computation.81 | loop fusion | flops 34603008 | bytes 18874384 | tf_op jit(solution)/shard_map/sub | solution.py:39
  71.1 8.6 %subtract_multiply_fusion.1 = (f32[512,1024]{1,0:T(8,128)}, f32[512,1024]{1,0:T(8,128)S(1)}, f32[512,1024]{1,0:T(8,128)}) fusion(f32[]{:T(128)} %bitcast.5, f32[]{:T(128)} %bitcast.4, f32[]{:T(128)} %bitcast.3, f32[1,1,8,512,1024]{4,3,2,1,0:T(8,128)} %param.5, f32[]{:T(128)} %bitcast.1, f32[512,1024]{1,0:T(8,128)} %get-tuple-element.16), kind=kLoop, calls=%fused_computation.333 | loop fusion | flops 17825792 | bytes 14680080 | tf_op jit(solution)/shard_map/mul | solution.py:37
  79.7 8.5 %subtract_multiply_fusion = (f32[512,1024]{1,0:T(8,128)}, f32[512,1024]{1,0:T(8,128)}) fusion(f32[]{:T(128)} %bitcast.5, f32[]{:T(128)} %bitcast.4, f32[]{:T(128)} %bitcast.3, f32[1,1,8,512,1024]{4,3,2,1,0:T(8,128)} %param.5, f32[]{:T(128)} %bitcast.1, f32[512,1024]{1,0:T(8,128)S(1)} %get-tuple-element.8), kind=kLoop, calls=%fused_computation.332 | loop fusion | flops 17825792 | bytes 12582928 | tf_op jit(solution)/shard_map/mul | solution.py:37
  88.9 23.5 %fusion.10 = f32[3,512,1024]{2,1,0:T(8,128)} fusion(f32[1,512,1024]{2,1,0:T(8,128)} %get-tuple-element.19, f32[1,512,1024]{2,1,0:T(8,128)} %get-tuple-element.20, f32[1,512,1024]{2,1,0:T(8,128)} %get-tuple-element.18, f32[1,512,1024]{2,1,0:T(8,128)} %get-tuple-element.22, f32[1,512,1024]{2,1,0:T(8,128)} %get-tuple-element.23, ...), kind=kLoop, calls=%fused_computation.14 | loop fusion | flops 86507520 | bytes 73400320 | tf_op jit(solution)/shard_map/add | solution.py:37
  112.4 4.4 %maximum_multiply_fusion = f32[4,512,1024]{2,1,0:T(8,128)S(1)} fusion(f32[1,512,1024]{2,1,0:T(8,128)} %fusion.56, f32[3,512,1024]{2,1,0:T(8,128)} %fusion.10, f32[]{:T(128)} %bitcast.33), kind=kLoop, calls=%fused_computation.2 | loop fusion | flops 4194304 | bytes 16777220 | tf_op jit(solution)/shard_map/mul | solution.py:40
  116.9 2.9 %dynamic-slice_bitcast_fusion = (f32[1,4,64,1024]{3,2,1,0:T(8,128)S(1)}, f32[1,4,64,1024]{3,2,1,0:T(8,128)S(1)}, f32[1,4,64,1024]{3,2,1,0:T(8,128)S(1)}, f32[1,4...) fusion(f32[4,512,1024]{2,1,0:T(8,128)S(1)} %maximum_multiply_fusi, ...), kind=kLoop, calls=%fused_computation.345 | loop fusion | bytes 14680092 | tf_op jit(solution)/shard_map/dynamic_slice | solution.py:16
  126.7 4.3 %broadcast_in_dim.21 = f32[8,4,64,1024]{3,2,1,0:T(8,128)} broadcast(f32[]{:T(128)} %constant.23.clone.1), dimensions={} | broadcast | bytes 8388612 | tf_op jit(solution)/shard_map/broadcast_in_dim | solution.py:14
  131.0 2.3 bitcast_dynamic-update-slice_fusion
  133.3 14.5 %collective-permute-done.1 = f32[1,4,64,1024]{3,2,1,0:T(8,128)} collective-permute-done((f32[1,4,64,1024]{3,2,1,0:T(8,128)}, f32[1,4,64,1024]{3,2,1,0:T(8,128)}, u32[]{:S(2)}, u32[]{:S(2)}) %collective-permute-start.1) | collective-permute-done | bytes 1048608 | tf_op jit(solution)/shard_map/ppermute | solution.py:18
  148.1 2.3 constant_dynamic-update-slice_fusion.6
  150.4 2.4 constant_dynamic-update-slice_fusion.5
  152.8 16.5 %collective-permute-done.2 = f32[1,4,64,1024]{3,2,1,0:T(8,128)} collective-permute-done((f32[1,4,64,1024]{3,2,1,0:T(8,128)}, f32[1,4,64,1024]{3,2,1,0:T(8,128)}, u32[]{:S(2)}, u32[]{:S(2)}) %collective-permute-start.2) | collective-permute-done | bytes 1048608 | tf_op jit(solution)/shard_map/ppermute | solution.py:18
  173.9 41.4 %collective-permute-done.4 = f32[1,4,64,1024]{3,2,1,0:T(8,128)} collective-permute-done((f32[1,4,64,1024]{3,2,1,0:T(8,128)S(1)}, f32[1,4,64,1024]{3,2,1,0:T(8,128)}, u32[]{:S(2)}, u32[]{:S(2)}) %collective-permute-start.4) | collective-permute-done | bytes 1048608 | tf_op jit(solution)/shard_map/ppermute | solution.py:18
  219.8 7.7 %gather_fusion = f32[8,4,64,1024]{3,2,1,0:T(8,128)} fusion(f32[8,4,64,1024]{3,2,1,0:T(8,128)} %constant_dynamic-update-slice_fusion, s32[1024]{0:T(1024)S(1)} %pad_clamp_fusion.1), kind=kCustom, calls=%fused_computation | custom fusion | bytes 16777248 | tf_op jit(solution)/shard_map/jit(_take)/gather | solution.py:49
  227.5 4.4 %broadcast_select_fusion = f32[8,4,64,1024]{3,2,1,0:T(8,128)S(1)} fusion(f32[8,4,64,1024]{3,2,1,0:T(8,128)} %gather_fusion, pred[8]{0:T(512)(128)(4,1)S(1)} %compare_and_fusion), kind=kLoop, calls=%fused_computation.51 | loop fusion | flops 2097152 | bytes 16777224 | tf_op jit(solution)/shard_map/jit(_take)/select_n | solution.py:49
  235.8 2.9 %reshape.1672 = f32[4,1,65536]{2,1,0:T(1,128)} reshape(f32[1024,1,4,64]{3,2,1,0:T(4,128)S(1)} %bitcast.740) | data formatting | bytes 2097152
  238.7 4.9 %all-to-all-start = ((f32[4,1,65536]{2,1,0:T(1,128)}), f32[4,1,65536]{2,1,0:T(1,128)S(1)}, u32[]{:S(2)}, u32[]{:S(2)}) async-start(f32[4,1,65536]{2,1,0:T(1,128)} %reshape.1672), calls=%async_computation | async-start | bytes 2097152 | tf_op jit(solution)/shard_map/all_to_all | solution.py:70
  243.7 26.7 %all-to-all-done = f32[4,1,65536]{2,1,0:T(1,128)S(1)} async-done(((f32[4,1,65536]{2,1,0:T(1,128)}), f32[4,1,65536]{2,1,0:T(1,128)S(1)}, u32[]{:S(2)}, u32[]{:S(2)}) %all-to-all-start) | async-done | bytes 1048608 | tf_op jit(solution)/shard_map/all_to_all | solution.py:70
  270.9 3.8 %reduce = f32[4,65536]{1,0:T(4,128)S(1)} reduce(f32[4,1,65536]{2,1,0:T(1,128)S(1)} %all-to-all-done, f32[]{:T(128)} %broadcast.1697), dimensions={1}, to_apply=%all_to_all.13.reduce_sub_computation | reduce | bytes 2097156 | tf_op jit(solution)/shard_map/all_to_all | solution.py:70
  (53 shorter events, 26.6 us)
Async XLA Ops:
  0.0 124.9 %copy-start = (s32[4,8]{1,0:T(4,128)S(1)}, s32[4,8]{1,0:T(4,128)}, u32[]{:S(2)}) copy-start(s32[4,8]{1,0:T(4,128)} %param.8) | copy-start | bytes 388
  2.0 16.1 %copy-start.1 = (f32[1,1,8,512,1024]{4,3,2,1,0:T(8,128)S(1)}, f32[1,1,8,512,1024]{4,3,2,1,0:T(8,128)}, u32[]{:S(2)}) copy-start(f32[1,1,8,512,1024]{4,3,2,1,0:T(8,128)} %param.5) | copy-start | bytes 50331652
  116.9 4.6 %copy-start.2 = (f32[4,512,1024]{2,1,0:T(8,128)}, f32[4,512,1024]{2,1,0:T(8,128)S(1)}, u32[]{:S(2)}) copy-start(f32[4,512,1024]{2,1,0:T(8,128)S(1)} %maximum_multiply_fusion) | copy-start | bytes 25165828
  121.4 3.7 %collective-permute-start = (f32[1,4,64,1024]{3,2,1,0:T(8,128)}, f32[1,4,64,1024]{3,2,1,0:T(8,128)}, u32[]{:S(2)}, u32[]{:S(2)}) collective-permute-start(f32[1,4,64,1024]{3,2,1,0:T(8,128)} %get-tuple-element.47), channel_id=1, source_target_pairs={{0,1},{1,0},{2,3},{3,2},{4,5},{5,4},{6,7},{7,6},{8,9},{9,8},{10,11... | collective-permute-start | bytes 3145736 | tf_op jit(solution)/shard_map/ppermute | solution.py:18
  121.4 26.3 %collective-permute-start.1 = (f32[1,4,64,1024]{3,2,1,0:T(8,128)}, f32[1,4,64,1024]{3,2,1,0:T(8,128)}, u32[]{:S(2)}, u32[]{:S(2)}) collective-permute-start(f32[1,4,64,1024]{3,2,1,0:T(8,128)} %get-tuple-element.46), channel_id=1, source_target_pairs={{0,2},{1,3},{2,0},{3,1},{4,6},{5,7},{6,4},{7,5},{8,10},{9,11},{10,... | collective-permute-start | bytes 3145736 | tf_op jit(solution)/shard_map/ppermute | solution.py:18
  121.4 47.9 %collective-permute-start.2 = (f32[1,4,64,1024]{3,2,1,0:T(8,128)}, f32[1,4,64,1024]{3,2,1,0:T(8,128)}, u32[]{:S(2)}, u32[]{:S(2)}) collective-permute-start(f32[1,4,64,1024]{3,2,1,0:T(8,128)} %get-tuple-element.45), channel_id=1, source_target_pairs={{0,3},{1,2},{2,1},{3,0},{4,7},{5,6},{6,5},{7,4},{8,11},{9,10},{10,... | collective-permute-start | bytes 3145736 | tf_op jit(solution)/shard_map/ppermute | solution.py:18
  123.3 48.3 %collective-permute-start.3 = (f32[1,4,64,1024]{3,2,1,0:T(8,128)}, f32[1,4,64,1024]{3,2,1,0:T(8,128)}, u32[]{:S(2)}, u32[]{:S(2)}) collective-permute-start(f32[1,4,64,1024]{3,2,1,0:T(8,128)} %get-tuple-element.44), channel_id=1, source_target_pairs={{0,4},{1,5},{2,6},{3,7},{4,0},{5,1},{6,2},{7,3},{8,12},{9,13},{10,... | collective-permute-start | bytes 3145736 | tf_op jit(solution)/shard_map/ppermute | solution.py:18
  124.8 90.5 %collective-permute-start.4 = (f32[1,4,64,1024]{3,2,1,0:T(8,128)S(1)}, f32[1,4,64,1024]{3,2,1,0:T(8,128)}, u32[]{:S(2)}, u32[]{:S(2)}) collective-permute-start(f32[1,4,64,1024]{3,2,1,0:T(8,128)S(1)} %get-tuple-element.43), channel_id=1, source_target_pairs={{0,5},{1,4},{2,7},{3,6},{4,1},{5,0},{6,3},{7,2},{8,13},{9,12},{10,... | collective-permute-start | bytes 3145736 | tf_op jit(solution)/shard_map/ppermute | solution.py:18
  125.1 92.5 %collective-permute-start.5 = (f32[1,4,64,1024]{3,2,1,0:T(8,128)S(1)}, f32[1,4,64,1024]{3,2,1,0:T(8,128)S(1)}, u32[]{:S(2)}, u32[]{:S(2)}) collective-permute-start(f32[1,4,64,1024]{3,2,1,0:T(8,128)S(1)} %get-tuple-element.42), channel_id=1, source_target_pairs={{0,6},{1,7},{2,4},{3,5},{4,2},{5,3},{6,0},{7,1},{8,14},{9,15},{10,... | collective-permute-start | bytes 3145736 | tf_op jit(solution)/shard_map/ppermute | solution.py:18
  147.8 71.0 %collective-permute-start.6 = (f32[1,4,64,1024]{3,2,1,0:T(8,128)S(1)}, f32[1,4,64,1024]{3,2,1,0:T(8,128)S(1)}, u32[]{:S(2)}, u32[]{:S(2)}) collective-permute-start(f32[1,4,64,1024]{3,2,1,0:T(8,128)S(1)} %get-tuple-element.41), channel_id=1, source_target_pairs={{0,7},{1,6},{2,5},{3,4},{4,3},{5,2},{6,1},{7,0},{8,15},{9,14},{10,... | collective-permute-start | bytes 3145736 | tf_op jit(solution)/shard_map/ppermute | solution.py:18
  235.8 7.8 %copy-start.3 = (s32[4]{0:T(128)S(1)}, s32[4]{0:T(128)}, u32[]{:S(2)}) copy-start(s32[4]{0:T(128)} %param.7) | copy-start | bytes 52
  238.7 31.7 %all-to-all-start = ((f32[4,1,65536]{2,1,0:T(1,128)}), f32[4,1,65536]{2,1,0:T(1,128)S(1)}, u32[]{:S(2)}, u32[]{:S(2)}) async-start(f32[4,1,65536]{2,1,0:T(1,128)} %reshape.1672), calls=%async_computation | async-start | bytes 2097152 | tf_op jit(solution)/shard_map/all_to_all | solution.py:70
